TPU v7x, 128 devices: a whole 4x4x4 slice. The times are simulated.
128 devices in a mesh: row: 8 (over y, core), col: 16 (over z, x).
Axes of the slice: x: 4, y: 4, z: 4, core: 2. Of those that a mesh axis runs over, the one named last changes fastest.
Arguments:
- ancestor_inverse: float32 [12288, 12288], P('row', 'col')
- factor: bfloat16 [3, 12288, 512], P(None, ('row', 'col')), may hold values from -0.5 to 0.5
- coupling: float32 [3, 512, 512], replicated, may hold values from -0.25 to 0.25
- diagonal_inverse: float32 [3, 512, 512], replicated, may hold values from -6 to 6
- ancestors: int32 [3, 24], replicated, may hold values from -1 to 23, as said below
Outputs:
- block_columns: float32 [3, 12288, 512], P(None, ('row', 'col'))
- block_rows: float32 [3, 12288, 512], P(None, ('col', 'row'))
- node_blocks: float32 [3, 3, 512, 512], replicated
Inputs may be any that keep to these rules, and one draw needn't show every extreme that they name: `ancestors`: row k lists the ancestor block rows of supernode k, blocks of 512 rows: distinct indices in increasing order, then -1 in the slots left. Every block is listed by some supernode.
All inputs are finite; a program needn't handle non-finite values.
Results may differ from a plain program's by a relative error of at most 0.0003.
Values may be sent and summed in bfloat16 or wider, within the bound.
A program may use at most 128 MiB of HBM per device.

v0:
```python
import jax
import jax.numpy as jnp
from jax import lax
from jax.sharding import PartitionSpec as P

highest = lax.Precision.HIGHEST


def broadcast(value, axis, source):
    kept = jnp.where(lax.axis_index(axis) == source, value, 0).astype(value.dtype)
    return lax.psum(kept, axis)


def matmul(left, right):
    return jnp.dot(left, right, precision=highest)


def left_dot(left, right):
    return lax.dot_general(left, right, (((0,), (0,)), ((), ())), precision=highest)


def pair_index(later, earlier):
    return later * (later - 1) // 2 + earlier


def local(ancestor_inverse, factor, coupling, diagonal_inverse, ancestors):
    col_count = lax.axis_size("col")
    row_count = lax.axis_size("row")
    row_index = lax.axis_index("row")
    col_index = lax.axis_index("col")
    nodes_total, piece_rows, sn_width = factor.shape
    rows_here, cols_here = ancestor_inverse.shape
    group_ratio = rows_here // cols_here
    first_row = (row_index * col_count + col_index) * piece_rows
    block_of_row = (first_row + jnp.arange(piece_rows, dtype=jnp.int32)) // sn_width
    source_row = col_index // group_ratio
    block_start = col_index % group_ratio * cols_here
    row_layout = []
    solved = {}
    for current in range(nodes_total):
        listed = jnp.any(ancestors[current][:, None] == block_of_row[None, :], axis=0)
        lower_part = jnp.where(listed[:, None], factor[current], jnp.zeros_like(factor[current]))
        lower_rows = lax.all_gather(lower_part, "col", axis=0, tiled=True)
        own_block = lax.dynamic_slice_in_dim(lower_rows, block_start, cols_here, 0)
        lower_cols = broadcast(own_block, "row", source_row).astype(jnp.float32)
        lower_here = lower_part.astype(jnp.float32)
        product_sum = lax.psum_scatter(
            matmul(ancestor_inverse, lower_cols), "col", scatter_dimension=0, tiled=True
        )
        for earlier in range(current):
            product_sum = product_sum + matmul(
                row_layout[earlier], coupling[pair_index(current, earlier)]
            )
        column = -product_sum
        stacked = jnp.concatenate(row_layout + [column], axis=1)
        summed = lax.psum(left_dot(lower_here, stacked), ("row", "col"))
        crosses = [
            summed[:, earlier * sn_width : (earlier + 1) * sn_width] for earlier in range(current)
        ]
        self_term = summed[:, current * sn_width : (current + 1) * sn_width]
        for earlier in range(current):
            block_value = -crosses[earlier].T
            for inner in range(current):
                block_value = block_value - matmul(
                    solved[earlier, inner], coupling[pair_index(current, inner)]
                )
            solved[earlier, current] = block_value
            solved[current, earlier] = block_value.T
        diag_value = diagonal_inverse[current] - self_term
        for earlier in range(current):
            diag_value = diag_value - left_dot(
                coupling[pair_index(current, earlier)], solved[earlier, current]
            )
        solved[current, current] = diag_value
        row_layout.append(column)
    finished = jnp.stack(row_layout)
    part_rows = piece_rows // row_count
    ratio_cols = col_count // row_count
    split_parts = finished.reshape(nodes_total, row_count, part_rows, sn_width)
    held = lax.all_to_all(split_parts, "row", split_axis=1, concat_axis=1, tiled=True)
    targets = jnp.arange(row_count, dtype=jnp.int32) * ratio_cols + col_index // row_count
    onehot = (targets[:, None] == jnp.arange(col_count, dtype=jnp.int32)[None, :]).astype(
        jnp.float32
    )
    slotted = jnp.einsum("rc,nrqs->ncqs", onehot, held, precision=highest)
    arrived = lax.all_to_all(slotted, "col", split_axis=1, concat_axis=1, tiled=True)
    picked = lax.dynamic_slice_in_dim(arrived, col_index % ratio_cols * row_count, row_count, 1)
    landed = lax.all_to_all(picked, "row", split_axis=1, concat_axis=1, tiled=True)
    mirrored_all = landed.reshape(nodes_total, piece_rows, sn_width)
    node_blocks = jnp.stack(
        [
            jnp.stack([solved[first_node, second_node] for second_node in range(nodes_total)])
            for first_node in range(nodes_total)
        ]
    )
    return (finished, mirrored_all, node_blocks)


def solution(mesh):
    placed = (P("row", "col"), P(None, ("row", "col"), None), P(), P(), P())
    return jax.shard_map(
        local,
        mesh=mesh,
        in_specs=placed,
        out_specs=(P(None, ("row", "col"), None), P(None, ("col", "row"), None), P()),
        check_vma=False,
    )
```

profile of v0, /device:TPU:1, one launch (start us, length us, event | category | flops | bytes accessed | tf_op | source)
XLA Modules:
  0.0 691.0 jit_solution(10552824575240240170)
XLA Ops:
  11.5 45.6 %all-gather.6.cloned.1.call-done = bf16[1536,512]{1,0:T(8,128)(2,1)} async-done(((bf16[96,512]{1,0:T(8,128)(2,1)}), bf16[1536,512]{1,0:T(8,128)(2,1)}) %all-gather.6.cloned.1.call-update) | async-done | bytes 1572880 | tf_op jit(solution)/shard_map/all_gather | solution.py:43
  59.2 43.3 %all-gather.4.cloned.1.call-done = bf16[1536,512]{1,0:T(8,128)(2,1)} async-done(((bf16[96,512]{1,0:T(8,128)(2,1)}), bf16[1536,512]{1,0:T(8,128)(2,1)}) %all-gather.4.cloned.1.call-update) | async-done | bytes 1572880 | tf_op jit(solution)/shard_map/all_gather | solution.py:43
  104.7 43.3 %all-gather.8.cloned.1.call-done = bf16[1536,512]{1,0:T(8,128)(2,1)} async-done(((bf16[96,512]{1,0:T(8,128)(2,1)}), bf16[1536,512]{1,0:T(8,128)(2,1)}) %all-gather.8.cloned.1.call-update) | async-done | bytes 1572880 | tf_op jit(solution)/shard_map/all_gather | solution.py:43
  150.3 66.0 %all-reduce.7.cloned.1.call-done = (bf16[768,512]{1,0:T(8,128)(2,1)}, bf16[768,512]{1,0:T(8,128)(2,1)}, bf16[768,512]{1,0:T(8,128)(2,1)}) async-done(((bf16[768,512]{1,0:T(8,128)(2,1)}, bf16[768,512]{1,0:T(8,128)(2,1)}, bf16[768,512]{1,0:T(8,128)(2,1)}), (bf16[768,512]{1,0:T(8,128)(2,1)}, bf16[768,512]{1,0:T(8,128)(2,1)}, bf16[768,512]{1,0:T(8,128)(2,1)})) %all-reduce.7.cloned.1.call-update) | async-done | bytes 2359312 | tf_op jit(solution)/shard_map/psum | solution.py:11
  216.2 6.7 convolution_bitcast_fusion.2
  225.3 6.7 convolution_bitcast_fusion.1
  234.5 6.7 convolution_bitcast_fusion
  244.1 57.1 %reduce-scatter.10.cloned.1.call-done = f32[96,512]{1,0:T(8,128)} async-done(((f32[1536,512]{1,0:T(8,128)}), f32[96,512]{1,0:T(8,128)}) %reduce-scatter.10.cloned.1.call-update) | async-done | bytes 196624 | tf_op jit(solution)/shard_map/reduce_scatter | solution.py:47
  301.2 78.3 %reduce-scatter.12.cloned.1.call-done = f32[96,512]{1,0:T(8,128)} async-done(((f32[1536,512]{1,0:T(8,128)}), f32[96,512]{1,0:T(8,128)}) %reduce-scatter.12.cloned.1.call-update) | async-done | bytes 196624 | tf_op jit(solution)/shard_map/reduce_scatter | solution.py:47
  381.3 77.3 %reduce-scatter.14.cloned.1.call-done = f32[96,512]{1,0:T(8,128)} async-done(((f32[1536,512]{1,0:T(8,128)}), f32[96,512]{1,0:T(8,128)}) %reduce-scatter.14.cloned.1.call-update) | async-done | bytes 196624 | tf_op jit(solution)/shard_map/reduce_scatter | solution.py:47
  464.2 3.1 fusion.38
  475.2 6.7 all-to-all-start
  481.9 15.6 %all-to-all-done = f32[3,8,12,512]{3,2,0,1:T(8,128)} async-done(((f32[3,8,12,512]{3,2,0,1:T(8,128)}), f32[3,8,12,512]{3,2,0,1:T(8,128)}, u32[]{:S(2)}, u32[]{:S(2)}) %all-to-all-start) | async-done | bytes 589856 | tf_op jit(solution)/shard_map/all_to_all | solution.py:80
  501.5 4.8 all-to-all-start.1
  506.3 21.0 %all-to-all-done.1 = f32[3,16,12,512]{3,2,0,1:T(8,128)} async-done(((f32[3,16,12,512]{3,2,0,1:T(8,128)}), f32[3,16,12,512]{3,2,0,1:T(8,128)}, u32[]{:S(2)}, u32[]{:S(2)}) %all-to-all-start.1) | async-done | bytes 1179680 | tf_op jit(solution)/shard_map/all_to_all | solution.py:86
  529.4 9.0 %all-to-all-start.2 = ((f32[3,8,12,512]{3,2,0,1:T(8,128)}), f32[3,8,12,512]{3,2,0,1:T(8,128)}, u32[]{:S(2)}, u32[]{:S(2)}) async-start(f32[3,8,12,512]{3,2,0,1:T(8,128)} %constant_dynamic-slice_fusion), calls=%async_computation.2 | async-start | bytes 1572864 | tf_op jit(solution)/shard_map/all_to_all | solution.py:88
  545.1 5.7 all-to-all-done.2
  555.1 83.9 %all-reduce.5.cloned.1.call-done = (f32[512,1536]{1,0:T(8,128)}, f32[512,512]{1,0:T(8,128)}, f32[512,1024]{0,1:T(8,128)}) async-done(((f32[512,1536]{1,0:T(8,128)}, f32[512,512]{1,0:T(8,128)}, f32[512,1024]{0,1:T(8,128)}), (f32[512,1536]{1,0:T(8,128)}, f32[512,512]{1,0:T(8,128)}, f32[512,1024]{0,1:T(8,128)})) %all-reduce.5.cloned.1.call-update) | async-done | bytes 6291472 | tf_op jit(solution)/shard_map/psum | solution.py:56
  638.9 3.8 bitcast_subtract_fusion.7
  653.7 3.1 fusion.2
  663.9 3.8 maximum_bitcast_fusion.1
  667.8 3.6 copy.95
  671.3 4.3 fusion.1
  679.1 4.9 pad_maximum_fusion
  (102 shorter events, 72.2 us)
Async XLA Ops:
  7.2 49.9 %all-gather.6.cloned.1.call-start = ((), (), s32[]{:S(2)}) async-start(), calls=%async_computation.7 | async-start | bytes 1671168 | tf_op jit(solution)/shard_map/all_gather | solution.py:43
  9.9 92.6 %all-gather.4.cloned.1.call-start = ((), (), s32[]{:S(2)}) async-start(), calls=%async_computation.6 | async-start | bytes 1671168 | tf_op jit(solution)/shard_map/all_gather | solution.py:43
  10.7 137.4 %all-gather.8.cloned.1.call-start = ((), (), s32[]{:S(2)}) async-start(), calls=%async_computation.8 | async-start | bytes 1671168 | tf_op jit(solution)/shard_map/all_gather | solution.py:43
  11.4 204.8 %all-reduce.7.cloned.1.call-start = ((), (), s32[]{:S(2)}) async-start(), calls=%async_computation.13 | async-start | bytes 4718592 | tf_op jit(solution)/shard_map/psum | solution.py:11
  150.2 151.0 %reduce-scatter.10.cloned.1.call-start = ((), (), s32[]{:S(2)}) async-start(), calls=%async_computation.9 | async-start | bytes 3342336 | tf_op jit(solution)/shard_map/reduce_scatter | solution.py:47
  225.3 154.3 %reduce-scatter.12.cloned.1.call-start = ((), (), s32[]{:S(2)}) async-start(), calls=%async_computation.10 | async-start | bytes 3342336 | tf_op jit(solution)/shard_map/reduce_scatter | solution.py:47
  234.4 224.1 %reduce-scatter.14.cloned.1.call-start = ((), (), s32[]{:S(2)}) async-start(), calls=%async_computation.11 | async-start | bytes 3342336 | tf_op jit(solution)/shard_map/reduce_scatter | solution.py:47
  243.6 136.0 %copy-start = (f32[3,512,512]{2,1,0:T(8,128)S(1)}, f32[3,512,512]{2,1,0:T(8,128)}, u32[]{:S(2)}) copy-start(f32[3,512,512]{2,1,0:T(8,128)} %param.7) | copy-start | bytes 9437188
  243.6 395.3 %all-reduce.5.cloned.1.call-start = ((), (), s32[]{:S(2)}) async-start(), calls=%async_computation.12 | async-start | bytes 12582912 | tf_op jit(solution)/shard_map/psum | solution.py:56
  301.2 159.9 %copy-start.16 = (f32[96,512]{1,0:T(8,128)S(1)}, f32[96,512]{1,0:T(8,128)}, u32[]{:S(2)}) copy-start(f32[96,512]{1,0:T(8,128)} %reduce-scatter.10.cloned.1.call-done) | copy-start | bytes 589828
  458.6 5.7 copy-start.22
  461.1 6.2 copy-start.17
  461.9 5.5 copy-start.19
  461.9 5.5 copy-start.21
  475.2 22.3 %all-to-all-start = ((f32[3,8,12,512]{3,2,0,1:T(8,128)}), f32[3,8,12,512]{3,2,0,1:T(8,128)}, u32[]{:S(2)}, u32[]{:S(2)}) async-start(f32[3,8,12,512]{3,2,0,1:T(8,128)} %copy.78), calls=%async_computation | async-start | bytes 1572864 | tf_op jit(solution)/shard_map/all_to_all | solution.py:80
  501.5 25.8 %all-to-all-start.1 = ((f32[3,16,12,512]{3,2,0,1:T(8,128)}), f32[3,16,12,512]{3,2,0,1:T(8,128)}, u32[]{:S(2)}, u32[]{:S(2)}) async-start(f32[3,16,12,512]{3,2,0,1:T(8,128)} %copy.80), calls=%async_computation.1 | async-start | bytes 3145728 | tf_op jit(solution)/shard_map/all_to_all | solution.py:86
  529.4 21.4 %all-to-all-start.2 = ((f32[3,8,12,512]{3,2,0,1:T(8,128)}), f32[3,8,12,512]{3,2,0,1:T(8,128)}, u32[]{:S(2)}, u32[]{:S(2)}) async-start(f32[3,8,12,512]{3,2,0,1:T(8,128)} %constant_dynamic-slice_fusion), calls=%async_computation.2 | async-start | bytes 1572864 | tf_op jit(solution)/shard_map/all_to_all | solution.py:88
  642.7 5.8 copy-start.1
  646.6 12.5 %copy-start.3 = (f32[512,512]{0,1:T(8,128)}, f32[512,512]{0,1:T(8,128)S(1)}, u32[]{:S(2)}) copy-start(f32[512,512]{0,1:T(8,128)S(1)} %fusion.18) | copy-start | bytes 3145732
  648.5 5.1 copy-start.6
  653.7 5.4 copy-start.4
  671.3 4.3 copy-start.2
  671.3 4.3 copy-start.12
  671.3 4.3 copy-start.15
  (10 other events, 25.4 us)
Sparse Core Ops, SparseCore 0:
  10.7 46.3 all-gather.5
  59.2 43.3 all-gather.3
  104.7 43.3 all-gather.7
  151.0 65.1 all-reduce.6
  225.4 75.7 reduce-scatter.9
  304.4 75.1 reduce-scatter.11
  383.4 75.0 reduce-scatter.13
  469.1 169.7 all-reduce.4
where the time goes:
time: 699 us; the launch traced here: 691 us
  waiting for transfers between devices  539 us (77%)
  matrix products  54.5 us (8%)
  local copies, waits for them, and re-layouts  36 us (5%)
  other arithmetic  26 us (4%)
  starting transfers between devices  21.2 us (3%)
  between operations  14.7 us (2%)
    reduce_scatter x3, waiting for transfers between devices, local(): lax.psum_scatter(matmul(ancestor_inverse, lower_cols), 'col', scatter_dim...  213 us
    all_gather x3, waiting for transfers between devices, local(): lower_rows = lax.all_gather(lower_part, 'col', axis=0, tiled=True)  132 us
    psum x1, waiting for transfers between devices, local(): summed = lax.psum(left_dot(lower_here, stacked), ('row', 'col'))  83.9 us
    psum x1, waiting for transfers between devices, broadcast(): return lax.psum(kept, axis)  66 us
    dot_general x11, matrix products, matmul(): return jnp.dot(left, right, precision=highest)  36 us
    all_to_all x1, waiting for transfers between devices, local(): lax.all_to_all(slotted, 'col', split_axis=1, concat_axis=1, tiled=True)  21 us
    dot_general x6, matrix products, left_dot(): lax.dot_general(left, right, (((0,), (0,)), ((), ())), precision=highest)  16.5 us
    all_to_all x1, waiting for transfers between devices, local(): lax.all_to_all(split_parts, 'row', split_axis=1, concat_axis=1, tiled=True)  15.6 us
  transfers between devices with their start and end apart: 11, of which 11 were waited for; matrix products, arithmetic and copies ran while one was open for 7% of the time, Pallas kernels for 0%

commit v1 on v0

--- a/solution.py
+++ b/solution.py
@@ -53,7 +53,7 @@
             )
         column = -product_sum
         stacked = jnp.concatenate(row_layout + [column], axis=1)
-        summed = lax.psum(left_dot(lower_here, stacked), ("row", "col"))
+        summed = lax.psum(lax.psum(left_dot(lower_here, stacked), "col"), "row")
         crosses = [
             summed[:, earlier * sn_width : (earlier + 1) * sn_width] for earlier in range(current)
         ]

time: 699 us -> 757 us (1.083)
  waiting for transfers between devices: 539 us -> 600 us
    psum x1 -> x2, waiting for transfers between devices: 83.9 us -> 138 us  [local(): summed = lax.psum(lax.psum(left_dot(lower_here, stacked), 'col'), 'row')]
  transfers between devices with their start and end apart: 11 -> 12, of which waited for: 11 -> 12; matrix products, arithmetic and copies ran while one was open for 7% -> 6% of each run, Pallas kernels for 0% -> 0%
where the time goes in v1:
time: 757 us; the launch traced here: 748 us
  waiting for transfers between devices  600 us (79%)
  matrix products  54.6 us (7%)
  local copies, waits for them, and re-layouts  35.7 us (5%)
  other arithmetic  25.9 us (3%)
  starting transfers between devices  18.2 us (2%)
  between operations  14.5 us (2%)
    reduce_scatter x3, waiting for transfers between devices, local(): lax.psum_scatter(matmul(ancestor_inverse, lower_cols), 'col', scatter_dim...  213 us
    psum x2, waiting for transfers between devices, local(): summed = lax.psum(lax.psum(left_dot(lower_here, stacked), 'col'), 'row')  138 us
    all_gather x3, waiting for transfers between devices, local(): lower_rows = lax.all_gather(lower_part, 'col', axis=0, tiled=True)  132 us
    psum x1, waiting for transfers between devices, broadcast(): return lax.psum(kept, axis)  66 us
    dot_general x11, matrix products, matmul(): return jnp.dot(left, right, precision=highest)  36 us
    all_to_all x1, waiting for transfers between devices, local(): lax.all_to_all(slotted, 'col', split_axis=1, concat_axis=1, tiled=True)  22.1 us
    all_to_all x1, waiting for transfers between devices, local(): lax.all_to_all(split_parts, 'row', split_axis=1, concat_axis=1, tiled=True)  16.7 us
    dot_general x6, matrix products, left_dot(): lax.dot_general(left, right, (((0,), (0,)), ((), ())), precision=highest)  16.5 us
  transfers between devices with their start and end apart: 12, of which 12 were waited for; matrix products, arithmetic and copies ran while one was open for 6% of the time, Pallas kernels for 0%

profile of v1, /device:TPU:1, one launch (start us, length us, event | category | flops | bytes accessed | tf_op | source)
XLA Modules:
  0.0 748.4 jit_solution(15477927722143181249)
XLA Ops:
  11.5 45.6 %all-gather.6.cloned.1.call-done = bf16[1536,512]{1,0:T(8,128)(2,1)} async-done(((bf16[96,512]{1,0:T(8,128)(2,1)}), bf16[1536,512]{1,0:T(8,128)(2,1)}) %all-gather.6.cloned.1.call-update) | async-done | bytes 1572880 | tf_op jit(solution)/shard_map/all_gather | solution.py:43
  59.2 43.3 %all-gather.4.cloned.1.call-done = bf16[1536,512]{1,0:T(8,128)(2,1)} async-done(((bf16[96,512]{1,0:T(8,128)(2,1)}), bf16[1536,512]{1,0:T(8,128)(2,1)}) %all-gather.4.cloned.1.call-update) | async-done | bytes 1572880 | tf_op jit(solution)/shard_map/all_gather | solution.py:43
  104.7 43.4 %all-gather.8.cloned.1.call-done = bf16[1536,512]{1,0:T(8,128)(2,1)} async-done(((bf16[96,512]{1,0:T(8,128)(2,1)}), bf16[1536,512]{1,0:T(8,128)(2,1)}) %all-gather.8.cloned.1.call-update) | async-done | bytes 1572880 | tf_op jit(solution)/shard_map/all_gather | solution.py:43
  150.3 66.0 %all-reduce.11.cloned.1.call-done = (bf16[768,512]{1,0:T(8,128)(2,1)}, bf16[768,512]{1,0:T(8,128)(2,1)}, bf16[768,512]{1,0:T(8,128)(2,1)}) async-done(((bf16[768,512]{1,0:T(8,128)(2,1)}, bf16[768,512]{1,0:T(8,128)(2,1)}, bf16[768,512]{1,0:T(8,128)(2,1)}), (bf16[768,512]{1,0:T(8,128)(2,1)}, bf16[768,512]{1,0:T(8,128)(2,1)}, bf16[768,512]{1,0:T(8,128)(2,1)})) %all-reduce.11.cloned.1.call-update) | async-done | bytes 2359312 | tf_op jit(solution)/shard_map/psum | solution.py:11
  216.2 6.7 convolution_bitcast_fusion.2
  225.3 6.7 convolution_bitcast_fusion.1
  234.5 6.7 convolution_bitcast_fusion
  244.1 57.1 %reduce-scatter.10.cloned.1.call-done = f32[96,512]{1,0:T(8,128)} async-done(((f32[1536,512]{1,0:T(8,128)}), f32[96,512]{1,0:T(8,128)}) %reduce-scatter.10.cloned.1.call-update) | async-done | bytes 196624 | tf_op jit(solution)/shard_map/reduce_scatter | solution.py:47
  301.2 78.3 %reduce-scatter.12.cloned.1.call-done = f32[96,512]{1,0:T(8,128)} async-done(((f32[1536,512]{1,0:T(8,128)}), f32[96,512]{1,0:T(8,128)}) %reduce-scatter.12.cloned.1.call-update) | async-done | bytes 196624 | tf_op jit(solution)/shard_map/reduce_scatter | solution.py:47
  381.3 77.2 %reduce-scatter.14.cloned.1.call-done = f32[96,512]{1,0:T(8,128)} async-done(((f32[1536,512]{1,0:T(8,128)}), f32[96,512]{1,0:T(8,128)}) %reduce-scatter.14.cloned.1.call-update) | async-done | bytes 196624 | tf_op jit(solution)/shard_map/reduce_scatter | solution.py:47
  469.0 123.7 %all-reduce.7.cloned.1.call-done = (f32[512,1536]{1,0:T(8,128)}, f32[512,512]{1,0:T(8,128)}, f32[512,1024]{0,1:T(8,128)}) async-done(((f32[512,1536]{1,0:T(8,128)}, f32[512,512]{1,0:T(8,128)}, f32[512,1024]{0,1:T(8,128)}), (f32[512,1536]{1,0:T(8,128)}, f32[512,512]{1,0:T(8,128)}, f32[512,1024]{0,1:T(8,128)})) %all-reduce.7.cloned.1.call-update) | async-done | bytes 6291472 | tf_op jit(solution)/shard_map/psum | solution.py:56
  598.9 5.0 all-to-all-start
  603.9 16.7 %all-to-all-done = f32[3,8,12,512]{3,2,0,1:T(8,128)} async-done(((f32[3,8,12,512]{3,2,0,1:T(8,128)}), f32[3,8,12,512]{3,2,0,1:T(8,128)}, u32[]{:S(2)}, u32[]{:S(2)}) %all-to-all-start) | async-done | bytes 589856 | tf_op jit(solution)/shard_map/all_to_all | solution.py:80
  624.6 5.0 all-to-all-start.1
  629.6 22.1 %all-to-all-done.1 = f32[3,16,12,512]{3,2,0,1:T(8,128)} async-done(((f32[3,16,12,512]{3,2,0,1:T(8,128)}), f32[3,16,12,512]{3,2,0,1:T(8,128)}, u32[]{:S(2)}, u32[]{:S(2)}) %all-to-all-start.1) | async-done | bytes 1179680 | tf_op jit(solution)/shard_map/all_to_all | solution.py:86
  653.8 7.5 all-to-all-start.2
  667.9 10.0 %all-to-all-done.2 = f32[3,8,12,512]{3,2,0,1:T(8,128)} async-done(((f32[3,8,12,512]{3,2,0,1:T(8,128)}), f32[3,8,12,512]{3,2,0,1:T(8,128)}, u32[]{:S(2)}, u32[]{:S(2)}) %all-to-all-start.2) | async-done | bytes 589856 | tf_op jit(solution)/shard_map/all_to_all | solution.py:88
  682.0 14.6 %all-reduce.9.cloned.1.call-done = (f32[512,1536]{1,0:T(8,128)}, f32[512,512]{1,0:T(8,128)}, f32[512,1024]{0,1:T(8,128)}) async-done(((f32[512,1536]{1,0:T(8,128)}, f32[512,512]{1,0:T(8,128)}, f32[512,1024]{0,1:T(8,128)}), (f32[512,1536]{1,0:T(8,128)}, f32[512,512]{1,0:T(8,128)}, f32[512,1024]{0,1:T(8,128)})) %all-reduce.9.cloned.1.call-update) | async-done | bytes 6291472 | tf_op jit(solution)/shard_map/psum | solution.py:56
  696.6 3.8 bitcast_subtract_fusion.7
  711.4 3.1 fusion.2
  721.7 3.8 maximum_bitcast_fusion.1
  725.5 3.5 copy.95
  729.0 4.3 fusion.1
  736.8 4.9 pad_maximum_fusion
  (105 shorter events, 75.1 us)
Async XLA Ops:
  7.2 49.9 %all-gather.6.cloned.1.call-start = ((), (), s32[]{:S(2)}) async-start(), calls=%async_computation.7 | async-start | bytes 1671168 | tf_op jit(solution)/shard_map/all_gather | solution.py:43
  9.9 92.6 %all-gather.4.cloned.1.call-start = ((), (), s32[]{:S(2)}) async-start(), calls=%async_computation.6 | async-start | bytes 1671168 | tf_op jit(solution)/shard_map/all_gather | solution.py:43
  10.7 137.4 %all-gather.8.cloned.1.call-start = ((), (), s32[]{:S(2)}) async-start(), calls=%async_computation.8 | async-start | bytes 1671168 | tf_op jit(solution)/shard_map/all_gather | solution.py:43
  11.4 204.8 %all-reduce.11.cloned.1.call-start = ((), (), s32[]{:S(2)}) async-start(), calls=%async_computation.14 | async-start | bytes 4718592 | tf_op jit(solution)/shard_map/psum | solution.py:11
  150.2 151.0 %reduce-scatter.10.cloned.1.call-start = ((), (), s32[]{:S(2)}) async-start(), calls=%async_computation.9 | async-start | bytes 3342336 | tf_op jit(solution)/shard_map/reduce_scatter | solution.py:47
  225.3 154.3 %reduce-scatter.12.cloned.1.call-start = ((), (), s32[]{:S(2)}) async-start(), calls=%async_computation.10 | async-start | bytes 3342336 | tf_op jit(solution)/shard_map/reduce_scatter | solution.py:47
  234.5 224.1 %reduce-scatter.14.cloned.1.call-start = ((), (), s32[]{:S(2)}) async-start(), calls=%async_computation.11 | async-start | bytes 3342336 | tf_op jit(solution)/shard_map/reduce_scatter | solution.py:47
  243.6 136.0 %copy-start = (f32[3,512,512]{2,1,0:T(8,128)S(1)}, f32[3,512,512]{2,1,0:T(8,128)}, u32[]{:S(2)}) copy-start(f32[3,512,512]{2,1,0:T(8,128)} %param.7) | copy-start | bytes 9437188
  243.6 349.2 %all-reduce.7.cloned.1.call-start = ((), (), s32[]{:S(2)}) async-start(), calls=%async_computation.12 | async-start | bytes 12582912 | tf_op jit(solution)/shard_map/psum | solution.py:56
  301.2 159.9 %copy-start.16 = (f32[96,512]{1,0:T(8,128)S(1)}, f32[96,512]{1,0:T(8,128)}, u32[]{:S(2)}) copy-start(f32[96,512]{1,0:T(8,128)} %reduce-scatter.10.cloned.1.call-done) | copy-start | bytes 589828
  458.6 5.7 copy-start.22
  461.1 6.2 copy-start.17
  461.8 5.5 copy-start.19
  461.8 5.5 copy-start.21
  469.0 227.6 %all-reduce.9.cloned.1.call-start = ((), (), s32[]{:S(2)}) async-start(), calls=%async_computation.13 | async-start | bytes 12582912 | tf_op jit(solution)/shard_map/psum | solution.py:56
  598.9 21.7 %all-to-all-start = ((f32[3,8,12,512]{3,2,0,1:T(8,128)}), f32[3,8,12,512]{3,2,0,1:T(8,128)}, u32[]{:S(2)}, u32[]{:S(2)}) async-start(f32[3,8,12,512]{3,2,0,1:T(8,128)} %copy.78), calls=%async_computation | async-start | bytes 1572864 | tf_op jit(solution)/shard_map/all_to_all | solution.py:80
  624.6 27.1 %all-to-all-start.1 = ((f32[3,16,12,512]{3,2,0,1:T(8,128)}), f32[3,16,12,512]{3,2,0,1:T(8,128)}, u32[]{:S(2)}, u32[]{:S(2)}) async-start(f32[3,16,12,512]{3,2,0,1:T(8,128)} %copy.80), calls=%async_computation.1 | async-start | bytes 3145728 | tf_op jit(solution)/shard_map/all_to_all | solution.py:86
  653.8 24.2 %all-to-all-start.2 = ((f32[3,8,12,512]{3,2,0,1:T(8,128)}), f32[3,8,12,512]{3,2,0,1:T(8,128)}, u32[]{:S(2)}, u32[]{:S(2)}) async-start(f32[3,8,12,512]{3,2,0,1:T(8,128)} %constant_dynamic-slice_fusion), calls=%async_computation.2 | async-start | bytes 1572864 | tf_op jit(solution)/shard_map/all_to_all | solution.py:88
  700.4 5.8 copy-start.1
  704.3 12.5 %copy-start.3 = (f32[512,512]{0,1:T(8,128)}, f32[512,512]{0,1:T(8,128)S(1)}, u32[]{:S(2)}) copy-start(f32[512,512]{0,1:T(8,128)S(1)} %fusion.18) | copy-start | bytes 3145732
  706.2 5.1 copy-start.6
  711.4 5.5 copy-start.4
  729.0 4.3 copy-start.12
  729.0 4.3 copy-start.15
  (11 other events, 29.7 us)
Sparse Core Ops, SparseCore 0:
  10.7 46.3 all-gather.5
  59.2 43.3 all-gather.3
  104.7 43.3 all-gather.7
  151.0 65.1 all-reduce.10
  225.4 75.7 reduce-scatter.9
  304.4 75.0 reduce-scatter.11
  383.4 75.0 reduce-scatter.13
  469.1 123.6 all-reduce.6
  595.5 101.1 all-reduce.8
